TPU v7x, 32 devices: a whole 2x2x4 slice. The times are simulated.
32 devices in a mesh: groups: 2 (over y), wide: 8 (over z, x), narrow: 2 (over core).
Axes of the slice: x: 2, y: 2, z: 4, core: 2. Of those that a mesh axis runs over, the one named last changes fastest.
Arguments:
- queries: bfloat16 [16384, 1024], P(('groups', 'wide', 'narrow')), parts along dimension 0, may hold values from -6 to 6
- latents: bfloat16 [256, 1024], P(('groups', 'wide', 'narrow')), parts along dimension 0
- norm_gains: float32 [2, 1024], replicated, may hold values from 0.5 to 1.5
- q_weight: bfloat16 [2, 1024, 1024], P(None, 'narrow'), may hold values from -0.1875 to 0.1875
- k_weight: bfloat16 [2, 1024, 1024], P(None, 'narrow'), may hold values from -0.1875 to 0.1875
- v_weight: bfloat16 [2, 1024, 1024], P(None, 'narrow'), may hold values from -0.1875 to 0.1875
- o_weight: bfloat16 [2, 1024, 1024], P(None, 'narrow'), may hold values from -0.1875 to 0.1875
Outputs:
- decoded: bfloat16 [16384, 1024], P(('groups', 'wide', 'narrow')), parts along dimension 0
There are 2 independent parts, one for each index of `groups`. A program takes and returns all parts, laid end to end along the dimension named above; an argument that names none is the same for every part. Nothing has to cross between parts.
All inputs are finite; a program needn't handle non-finite values.
Results may differ from a plain program's by a relative error of at most 0.025.
The roundings to bfloat16 on the way count: a program that leaves them out, or rounds other values in their place, can miss the bound.
Values may be sent and summed in bfloat16 or wider, within the bound.
A program may use at most 128 MiB of HBM per device.

v0:
```python
import math

import jax
import jax.numpy as jnp
from jax import lax
from jax.sharding import PartitionSpec as P

HEADS = 16
LAYERS = 2


def layer_norm(row_data, gain):
    values = row_data.astype(jnp.float32)
    center = values - jnp.mean(values, axis=-1, keepdims=True)
    spread = jnp.mean(center * center, axis=-1, keepdims=True)
    return (center * lax.rsqrt(spread + 1e-05) * gain).astype(jnp.bfloat16)


def accumulate(left_rows, panel_piece):
    return jnp.dot(left_rows, panel_piece, preferred_element_type=jnp.float32)


def project_queries(normed, panel):
    initial = jnp.zeros((normed.shape[0], panel.shape[1]), jnp.float32)

    def add_panel(running, panel_piece, row_start):
        return accumulate(normed, panel_piece)

    return add_panel(initial, lax.all_gather(panel, "narrow", axis=0, tiled=True), jnp.int32(0))


def project_output(attended, panel):
    initial = jnp.zeros((attended.shape[0], panel.shape[1]), jnp.float32)

    def add_panel(running, panel_piece, row_start):
        return accumulate(attended, panel_piece)

    return add_panel(initial, lax.all_gather(panel, "narrow", axis=0, tiled=True), jnp.int32(0))


def project_latents(source, key_panel, value_panel):
    key_sums = accumulate(source, lax.all_gather(key_panel, "narrow", axis=0, tiled=True))
    value_sums = accumulate(source, lax.all_gather(value_panel, "narrow", axis=0, tiled=True))
    return (key_sums.astype(jnp.bfloat16), value_sums.astype(jnp.bfloat16))


def attend_rows(carried, pieces, query_heads):
    key_rows, value_rows = pieces
    key_count = key_rows.shape[0]
    head_count = query_heads.shape[1]
    head_size = query_heads.shape[2]
    block_rows = math.gcd(key_count, 256)
    key_blocks = key_rows.reshape(key_count // block_rows, block_rows, head_count, head_size)
    value_blocks = value_rows.reshape(key_count // block_rows, block_rows, head_count, head_size)

    def fold_step(current, blocks_now):
        row_max, row_sum, weighted = current
        key_block, value_block = blocks_now
        scores = jnp.einsum(
            "qhd,khd->hqk", query_heads, key_block, preferred_element_type=jnp.float32
        )
        new_max = jnp.maximum(row_max, jnp.max(scores, axis=-1))
        rescale = jnp.exp(row_max - new_max)
        expo = jnp.exp(scores - new_max[:, :, None])
        row_sum = row_sum * rescale + jnp.sum(expo, axis=-1)
        mixed_sum = jnp.einsum(
            "hqk,khd->qhd",
            expo.astype(jnp.bfloat16),
            value_block,
            preferred_element_type=jnp.float32,
        )
        weighted = weighted * jnp.transpose(rescale)[:, :, None] + mixed_sum
        return ((new_max, row_sum, weighted), None)

    carried, unused = lax.scan(fold_step, carried, (key_blocks, value_blocks))
    return carried


def shards(queries, latents, norm_gains, q_weight, k_weight, v_weight, o_weight):
    query_count = queries.shape[0]
    model_width = queries.shape[1]
    head_count = HEADS
    head_size = model_width // head_count
    score_scale = head_size ** (-0.5)
    all_latents = lax.all_gather(latents, ("wide", "narrow"), axis=0, tiled=True)
    hidden = queries
    for layer_index in range(LAYERS):
        normed = layer_norm(hidden, norm_gains[layer_index])
        query_sums = project_queries(normed, q_weight[layer_index])
        query_rows = (query_sums * score_scale).astype(jnp.bfloat16)
        query_heads = query_rows.reshape(query_count, head_count, head_size)
        initial = (
            jnp.full((head_count, query_count), -1e30, jnp.float32),
            jnp.zeros((head_count, query_count), jnp.float32),
            jnp.zeros((query_count, head_count, head_size), jnp.float32),
        )
        key_rows, value_rows = project_latents(
            all_latents, k_weight[layer_index], v_weight[layer_index]
        )
        carried = attend_rows(initial, (key_rows, value_rows), query_heads)
        row_max, row_sum, weighted = carried
        attended = (
            (weighted / jnp.transpose(row_sum)[:, :, None])
            .reshape(query_count, model_width)
            .astype(jnp.bfloat16)
        )
        output_rows = project_output(attended, o_weight[layer_index])
        hidden = (hidden.astype(jnp.float32) + output_rows).astype(jnp.bfloat16)
    return hidden


def solution(mesh):
    return jax.shard_map(
        shards,
        mesh=mesh,
        in_specs=(
            P(("groups", "wide", "narrow"), None),
            P(("groups", "wide", "narrow"), None),
            P(),
            P(None, "narrow", None),
            P(None, "narrow", None),
            P(None, "narrow", None),
            P(None, "narrow", None),
        ),
        out_specs=P(("groups", "wide", "narrow"), None),
        check_vma=False,
    )
```

profile of v0, /device:TPU:0, one launch (start us, length us, event | category | flops | bytes accessed | tf_op | source)
XLA Modules:
  0.0 126.7 jit_solution(10234056180179298440)
XLA Ops:
  6.5 3.2 %fusion.77 = (bf16[1,512,1024]{2,1,0:T(8,128)(2,1)}, bf16[1,512,1024]{2,1,0:T(8,128)(2,1)}) fusion(bf16[2,512,1024]{2,1,0:T(8,128)(2,1)} %param.12), kind=kLoop, calls=%fused_computation.75 | loop fusion | bytes 4194304 | tf_op jit(solution)/shard_map/slice | solution.py:98
  9.8 1.5 %fusion.76 = (bf16[1,512,1024]{2,1,0:T(8,128)(2,1)}, bf16[1,512,1024]{2,1,0:T(8,128)(2,1)}) fusion(bf16[2,512,1024]{2,1,0:T(8,128)(2,1)S(1)} %copy-done.2), kind=kLoop, calls=%fused_computation.74 | loop fusion | bytes 4194304 | tf_op jit(solution)/shard_map/slice | solution.py:89
  11.4 3.1 %fusion.75 = (bf16[1,512,1024]{2,1,0:T(8,128)(2,1)}, bf16[1,512,1024]{2,1,0:T(8,128)(2,1)}) fusion(bf16[2,512,1024]{2,1,0:T(8,128)(2,1)} %param.11), kind=kLoop, calls=%fused_computation.73 | loop fusion | bytes 4194304 | tf_op jit(solution)/shard_map/slice | solution.py:98
  15.1 0.9 copy-done.3
  16.1 1.5 %fusion.74 = (bf16[1,512,1024]{2,1,0:T(8,128)(2,1)}, bf16[1,512,1024]{2,1,0:T(8,128)(2,1)}) fusion(bf16[2,512,1024]{2,1,0:T(8,128)(2,1)S(1)} %copy-done.3), kind=kLoop, calls=%fused_computation.72 | loop fusion | bytes 4194304 | tf_op jit(solution)/shard_map/slice | solution.py:107
  19.7 23.8 %all_gather.28 = bf16[128,1024]{1,0:T(8,128)(2,1)S(1)} all-gather(bf16[8,1024]{1,0:T(8,128)(2,1)S(1)} %copy-done.5), channel_id=1, replica_groups=mesh['groups'=2,'wide'=8,'narrow'=2] {'wide','narrow'}, dimensions={0}, use_global_device_ids=true | all-gather | bytes 278528 | tf_op jit(solution)/shard_map/all_gather | solution.py:85
  44.2 2.2 %fusion.57 = bf16[128,1024]{1,0:T(8,128)(2,1)S(1)} fusion(bf16[128,1024]{1,0:T(8,128)(2,1)S(1)} %all_gather.28, bf16[1,1024,1024]{2,1,0:T(8,128)(2,1)} %all-gather.21.cloned.1.call-done), kind=kOutput, calls=%fused_computation.53 | convolution fusion | flops 268566528 | bytes 2621440 | tf_op jit(solution)/shard_map/dot_general | solution.py:20
  46.4 0.9 copy.18
  47.3 3.2 %multiply_convert_fusion.1 = bf16[512,1024]{1,0:T(8,128)(2,1)S(1)} fusion(bf16[1,1024,1024]{2,1,0:T(8,128)(2,1)} %all-gather.17.cloned.1.call-done, bf16[512,1024]{1,0:T(8,128)(2,1)S(1)} %copy-done.1, f32[1024]{0:T(1024)S(1)} %bitcast.95, f32[512]{0:T(512)S(1)} %add_rsqrt_fusion.1, f32[512]{0:T(512)S(1)} %broadcast_multiply_fusion.1), kind=kOutput, calls=%fused_computation.51 | convolution fusion | flops 1077411840 | bytes 4202496 | tf_op jit(solution)/shard_map/dot_general | solution.py:20
  51.1 2.0 %fusion.54 = bf16[128,1024]{1,0:T(8,128)(2,1)S(1)} fusion(bf16[128,1024]{1,0:T(8,128)(2,1)S(1)} %all_gather.28, bf16[1,1024,1024]{2,1,0:T(8,128)(2,1)} %all-gather.19.cloned.1.call-done), kind=kOutput, calls=%fused_computation.52 | convolution fusion | flops 268566528 | bytes 2621440 | tf_op jit(solution)/shard_map/dot_general | solution.py:20
  54.8 1.2 copy-done
  56.0 7.0 %all-gather.29.cloned.1.call-done = bf16[1,1024,1024]{2,1,0:T(8,128)(2,1)} async-done(((bf16[1,512,1024]{2,1,0:T(8,128)(2,1)}), bf16[1,1024,1024]{2,1,0:T(8,128)(2,1)}) %all-gather.29.cloned.1.call-update) | async-done | bytes 2097168 | tf_op jit(solution)/shard_map/all_gather | solution.py:43
  63.1 2.0 %fusion.63 = bf16[128,1024]{1,0:T(8,128)(2,1)S(1)} fusion(bf16[128,1024]{1,0:T(8,128)(2,1)S(1)} %all_gather.28, bf16[1,1024,1024]{2,1,0:T(8,128)(2,1)} %all-gather.29.cloned.1.call-done), kind=kOutput, calls=%fused_computation.55 | convolution fusion | flops 268566528 | bytes 2621440 | tf_op jit(solution)/shard_map/dot_general | solution.py:20
  65.3 4.1 %fusion.33 = bf16[512,16,64]{0,2,1:T(8,128)(2,1)} fusion(bf16[128,16,64]{0,2,1:T(8,128)(2,1)S(1)} %bitcast.93, f32[16,512,128]{1,2,0:T(8,128)} %copy-done, f32[16,512]{1,0:T(8,128)S(1)} %get-tuple-element.56, f32[512,16]{0,1:T(8,128)S(1)} %bitcast_add_fusion.3, f32[512,16]{0,1:T(8,128)S(1)} %get-tuple-element.48), kind=kOutput, calls=%fused_computation.41 | convolution fusion | flops 137887744 | bytes 5603328 | tf_op jit(solution)/shard_map/while/body/eval_jaxpr/hqk,khd->qhd/dot_general | solution.py:66
  69.4 6.9 %all-gather.23.cloned.1.call-done = bf16[1,1024,1024]{2,1,0:T(8,128)(2,1)} async-done(((bf16[1,512,1024]{2,1,0:T(8,128)(2,1)}), bf16[1,1024,1024]{2,1,0:T(8,128)(2,1)}) %all-gather.23.cloned.1.call-update) | async-done | bytes 2097168 | tf_op jit(solution)/shard_map/all_gather | solution.py:38
  76.2 3.3 %convert_reduce_fusion = (f32[512]{0:T(512)S(1)}, bf16[512,1024]{1,0:T(8,128)(2,1)S(1)}) fusion(bf16[512,1024]{0,1:T(8,128)(2,1)} %bitcast.96, bf16[1,1024,1024]{2,1,0:T(8,128)(2,1)} %all-gather.23.cloned.1.call-done, bf16[512,1024]{1,0:T(8,128)(2,1)S(1)} %copy-done.1), kind=kOutput, calls=%fused_computation.8 | convolution fusion | flops 1076362752 | bytes 5244928 | tf_op jit(solution)/shard_map/dot_general | solution.py:20
  79.9 9.5 %all-gather.25.cloned.1.call-done = bf16[1,1024,1024]{2,1,0:T(8,128)(2,1)} async-done(((bf16[1,512,1024]{2,1,0:T(8,128)(2,1)}), bf16[1,1024,1024]{2,1,0:T(8,128)(2,1)}) %all-gather.25.cloned.1.call-update) | async-done | bytes 2097168 | tf_op jit(solution)/shard_map/all_gather | solution.py:29
  89.4 3.9 %multiply_convert_fusion = bf16[512,1024]{1,0:T(8,128)(2,1)} fusion(bf16[1,1024,1024]{2,1,0:T(8,128)(2,1)} %all-gather.25.cloned.1.call-done, bf16[512,1024]{1,0:T(8,128)(2,1)S(1)} %get-tuple-element.64, f32[1024]{0:T(1024)S(1)} %bitcast.94, f32[512]{0:T(512)S(1)} %add_rsqrt_fusion, f32[512]{0:T(512)S(1)} %broadcast_multiply_fusion), kind=kOutput, calls=%fused_computation.49 | convolution fusion | flops 1077411840 | bytes 4202496 | tf_op jit(solution)/shard_map/dot_general | solution.py:20
  93.3 1.5 %copy.20 = bf16[512,1024]{0,1:T(8,128)(2,1)S(1)} copy(bf16[512,1024]{1,0:T(8,128)(2,1)} %multiply_convert_fusion) | data formatting | bytes 2097152 | tf_op jit(solution)/shard_map/convert_element_type | solution.py:90
  94.8 8.0 %all-gather.27.cloned.1.call-done = bf16[1,1024,1024]{2,1,0:T(8,128)(2,1)} async-done(((bf16[1,512,1024]{2,1,0:T(8,128)(2,1)}), bf16[1,1024,1024]{2,1,0:T(8,128)(2,1)}) %all-gather.27.cloned.1.call-update) | async-done | bytes 2097168 | tf_op jit(solution)/shard_map/all_gather | solution.py:42
  102.7 2.0 %fusion.60 = bf16[128,1024]{1,0:T(8,128)(2,1)S(1)} fusion(bf16[128,1024]{1,0:T(8,128)(2,1)S(1)} %all_gather.28, bf16[1,1024,1024]{2,1,0:T(8,128)(2,1)} %all-gather.27.cloned.1.call-done), kind=kOutput, calls=%fused_computation.54 | convolution fusion | flops 268566528 | bytes 2621440 | tf_op jit(solution)/shard_map/dot_general | solution.py:20
  106.5 1.0 fusion.23
  107.5 8.6 %all-gather.31.cloned.1.call-done = bf16[1,1024,1024]{2,1,0:T(8,128)(2,1)} async-done(((bf16[1,512,1024]{2,1,0:T(8,128)(2,1)}), bf16[1,1024,1024]{2,1,0:T(8,128)(2,1)}) %all-gather.31.cloned.1.call-update) | async-done | bytes 2097168 | tf_op jit(solution)/shard_map/all_gather | solution.py:38
  116.1 3.8 %fusion.15 = bf16[512,1024]{1,0:T(8,128)(2,1)} fusion(bf16[512,1024]{1,0:T(8,128)(2,1)S(1)} %get-tuple-element.64, bf16[512,1024]{0,1:T(8,128)(2,1)S(1)} %bitcast.97, bf16[1,1024,1024]{2,1,0:T(8,128)(2,1)} %all-gather.31.cloned.1.call-done), kind=kOutput, calls=%fused_computation.23 | convolution fusion | flops 1075314688 | bytes 5242880 | tf_op jit(solution)/shard_map/dot_general | solution.py:20
  (51 shorter events, 8.0 us)
Async XLA Ops:
  6.5 3.3 %copy-start.2 = (bf16[2,512,1024]{2,1,0:T(8,128)(2,1)S(1)}, bf16[2,512,1024]{2,1,0:T(8,128)(2,1)}, u32[]{:S(2)}) copy-start(bf16[2,512,1024]{2,1,0:T(8,128)(2,1)} %param.10) | copy-start | bytes 6291460
  6.5 37.6 %all-gather.21.cloned.1.call-start = ((), (), s32[]{:S(2)}) async-start(), calls=%async_computation.2 | async-start | bytes 3145728 | tf_op jit(solution)/shard_map/all_gather | solution.py:43
  9.8 37.5 %all-gather.17.cloned.1.call-start = ((), (), s32[]{:S(2)}) async-start(), calls=%async_computation | async-start | bytes 3145728 | tf_op jit(solution)/shard_map/all_gather | solution.py:29
  11.3 39.7 %all-gather.19.cloned.1.call-start = ((), (), s32[]{:S(2)}) async-start(), calls=%async_computation.1 | async-start | bytes 3145728 | tf_op jit(solution)/shard_map/all_gather | solution.py:42
  14.5 1.6 %copy-start.3 = (bf16[2,512,1024]{2,1,0:T(8,128)(2,1)S(1)}, bf16[2,512,1024]{2,1,0:T(8,128)(2,1)}, u32[]{:S(2)}) copy-start(bf16[2,512,1024]{2,1,0:T(8,128)(2,1)} %param.13) | copy-start | bytes 6291460
  14.5 48.6 %all-gather.29.cloned.1.call-start = ((), (), s32[]{:S(2)}) async-start(), calls=%async_computation.6 | async-start | bytes 3145728 | tf_op jit(solution)/shard_map/all_gather | solution.py:43
  15.1 61.2 %all-gather.23.cloned.1.call-start = ((), (), s32[]{:S(2)}) async-start(), calls=%async_computation.3 | async-start | bytes 3145728 | tf_op jit(solution)/shard_map/all_gather | solution.py:38
  17.5 2.1 %copy-start.5 = (bf16[8,1024]{1,0:T(8,128)(2,1)S(1)}, bf16[8,1024]{1,0:T(8,128)(2,1)}, u32[]{:S(2)}) copy-start(bf16[8,1024]{1,0:T(8,128)(2,1)} %param.8) | copy-start | bytes 49156
  17.6 25.9 %copy-start.6 = (f32[2,1024]{1,0:T(2,128)S(1)}, f32[2,1024]{1,0:T(2,128)}, u32[]{:S(2)}) copy-start(f32[2,1024]{1,0:T(2,128)} %param.9) | copy-start | bytes 24580
  17.6 25.9 %copy-start.1 = (bf16[512,1024]{1,0:T(8,128)(2,1)S(1)}, bf16[512,1024]{1,0:T(8,128)(2,1)}, u32[]{:S(2)}) copy-start(bf16[512,1024]{1,0:T(8,128)(2,1)} %param.7) | copy-start | bytes 3145732
  17.6 71.8 %all-gather.25.cloned.1.call-start = ((), (), s32[]{:S(2)}) async-start(), calls=%async_computation.4 | async-start | bytes 3145728 | tf_op jit(solution)/shard_map/all_gather | solution.py:29
  18.2 84.6 %all-gather.27.cloned.1.call-start = ((), (), s32[]{:S(2)}) async-start(), calls=%async_computation.5 | async-start | bytes 3145728 | tf_op jit(solution)/shard_map/all_gather | solution.py:42
  18.9 97.2 %all-gather.31.cloned.1.call-start = ((), (), s32[]{:S(2)}) async-start(), calls=%async_computation.7 | async-start | bytes 3145728 | tf_op jit(solution)/shard_map/all_gather | solution.py:38
  54.1 2.0 %copy-start = (f32[16,512,128]{1,2,0:T(8,128)}, f32[16,512,128]{1,2,0:T(8,128)S(1)}, u32[]{:S(2)}) copy-start(f32[16,512,128]{1,2,0:T(8,128)S(1)} %get-tuple-element.62) | copy-start | bytes 12582916
  56.0 9.2 %copy-start.4 = (bf16[128,1024]{0,1:T(8,128)(2,1)S(1)}, bf16[128,1024]{0,1:T(8,128)(2,1)}, u32[]{:S(2)}) copy-start(bf16[128,1024]{0,1:T(8,128)(2,1)} %copy.18) | copy-start | bytes 786436
Sparse Core Ops, SparseCore 0:
  9.9 13.2 all-gather.20
  24.8 11.7 all-gather.16
  38.1 11.7 all-gather.18
  51.3 11.7 all-gather.28
  64.4 11.7 all-gather.22
  77.6 11.7 all-gather.24
  91.0 11.7 all-gather.26
  104.3 11.7 all-gather.30
where the time goes:
time: 127 us
  waiting for transfers between devices  42.4 us (33%)
  matrix products  29.1 us (23%)
  blocking collectives  23.8 us (19%)
  local copies, waits for them, and re-layouts  14.9 us (12%)
  between operations  13.7 us (11%)
  other arithmetic  2.53 us (2%)
    all_gather x1, blocking collectives, shards(): lax.all_gather(latents, ('wide', 'narrow'), axis=0, tiled=True)  23.8 us
    dot_general x8, matrix products, accumulate(): return jnp.dot(left_rows, panel_piece, preferred_element_type=jnp.float32)  22.5 us
    all_gather x2, waiting for transfers between devices, project_output(): lax.all_gather(panel, 'narrow', axis=0, tiled=True)  15.5 us
    all_gather x2, waiting for transfers between devices, project_queries(): lax.all_gather(panel, 'narrow', axis=0, tiled=True)  9.47 us
    all_gather x2, waiting for transfers between devices, project_latents(): lax.all_gather(key_panel, 'narrow', axis=0, tiled=True)  7.98 us
    all_gather x2, waiting for transfers between devices, project_latents(): lax.all_gather(value_panel, 'narrow', axis=0, tiled=True)  7.02 us
    dot_general x2, matrix products, fold_step(): jnp.einsum('hqk,khd->qhd', expo.astype(jnp.bfloat16), value_block, prefer...  5.08 us
    slice x1, local copies, waits for them, and re-layouts, shards(): v_weight[layer_index]  3.22 us
  transfers between devices with their start and end apart: 8, of which 5 were waited for; matrix products, arithmetic and copies ran while one was open for 29% of the time, Pallas kernels for 0%

commit v1 on v0

v1 whole, which is shorter than its diff:
```python
import functools

import jax
import jax.numpy as jnp
from jax import lax
from jax.experimental import pallas as pl
from jax.experimental.pallas import tpu as pltpu
from jax.sharding import PartitionSpec as P

HEADS = 16
LAYERS = 2
MESH = pl.DeviceIdType.MESH
F32 = jnp.float32
BF16 = jnp.bfloat16


def decoder(
    wide,
    narrow,
    queries,
    latents,
    gains,
    q_weight,
    k_weight,
    v_weight,
    o_weight,
    out,
    hidden,
    normed,
    query_rows,
    attended,
    lat,
    lat_rows,
    wq,
    wo,
    wk,
    wv,
    own_sums,
    peer_sums,
    local_sem,
    lat_local_sem,
    weight_local_sem,
    lat_send_sem,
    lat_recv_sem,
    weight_send_sem,
    weight_recv_sem,
    sums_send_sem,
    sums_recv_sem,
):
    devices = wide * narrow
    w = lax.axis_index("wide")
    n = lax.axis_index("narrow")
    me = w * narrow + n
    rows, width = hidden.shape
    half = wk.shape[1]
    lat_count = lat_rows.shape[0]
    head_size = width // HEADS
    pair = 2 * head_size
    scale = head_size ** (-0.5)
    my_half = pl.ds(pl.multiple_of(n * half, half), half)
    peer = {"narrow": 1 - n}

    local = [pltpu.make_async_copy(queries, hidden, local_sem)]
    own_latents = pltpu.make_async_copy(latents.at[:, my_half], lat.at[me], lat_local_sem)
    own = {}
    for layer in range(LAYERS):
        own["q", layer] = pltpu.make_async_copy(
            q_weight.at[layer], wq.at[layer, my_half], weight_local_sem.at[0, layer]
        )
        own["o", layer] = pltpu.make_async_copy(
            o_weight.at[layer], wo.at[layer, my_half], weight_local_sem.at[1, layer]
        )
        own["k", layer] = pltpu.make_async_copy(
            k_weight.at[layer], wk.at[layer], weight_local_sem.at[2, layer]
        )
        own["v", layer] = pltpu.make_async_copy(
            v_weight.at[layer], wv.at[layer], weight_local_sem.at[3, layer]
        )
    local[0].start()
    own_latents.start()
    for layer in range(LAYERS):
        for name in "kvqo":
            own[name, layer].start()

    barrier = pltpu.get_barrier_semaphore()

    def greet(step, carry):
        other = lax.rem(me + step, devices)
        pl.semaphore_signal(
            barrier,
            inc=1,
            device_id={"wide": other // narrow, "narrow": lax.rem(other, narrow)},
            device_id_type=MESH,
        )
        return carry

    lax.fori_loop(1, devices, greet, 0)
    pl.semaphore_wait(barrier, devices - 1)

    def latent_copy(step):
        other = lax.rem(me + step, devices)
        other_n = lax.rem(other, narrow)
        columns = pl.ds(pl.multiple_of(other_n * half, half), half)
        return pltpu.make_async_remote_copy(
            src_ref=latents.at[:, columns],
            dst_ref=lat.at[me],
            send_sem=lat_send_sem.at[step],
            recv_sem=lat_recv_sem.at[me],
            device_id={"wide": other // narrow, "narrow": other_n},
            device_id_type=MESH,
        )

    def send_latents(step, carry):
        latent_copy(step).start()
        return carry

    lax.fori_loop(1, devices, send_latents, 0)

    def weight_copy(index, layer):
        source, target = ((q_weight, wq), (o_weight, wo))[index]
        return pltpu.make_async_remote_copy(
            src_ref=source.at[layer],
            dst_ref=target.at[layer, my_half],
            send_sem=weight_send_sem.at[index, layer],
            recv_sem=weight_recv_sem.at[index, layer],
            device_id=peer,
            device_id_type=MESH,
        )

    def sums_copy(index, layer):
        return pltpu.make_async_remote_copy(
            src_ref=own_sums.at[layer, index],
            dst_ref=peer_sums.at[layer, index],
            send_sem=sums_send_sem.at[index, layer],
            recv_sem=sums_recv_sem.at[index, layer],
            device_id=peer,
            device_id_type=MESH,
        )

    weight_copy(0, 0).start()

    norm_rows = min(rows, 128)

    def layer_norm(layer):
        gain = gains[layer : layer + 1, :]

        def chunk(index, carry):
            piece = pl.ds(pl.multiple_of(index * norm_rows, norm_rows), norm_rows)
            values = hidden[piece, :].astype(F32)
            center = values - jnp.mean(values, axis=-1, keepdims=True)
            spread = jnp.mean(center * center, axis=-1, keepdims=True)
            normed[piece, :] = (center * lax.rsqrt(spread + 1e-05) * gain).astype(BF16)
            return carry

        lax.fori_loop(0, rows // norm_rows, chunk, 0)

    sum_rows = min(lat_count, 256)
    tile = 256

    def project_latents(index, layer):
        panel = (wk, wv)[index]

        def chunk(step, carry):
            row = step // (width // tile)
            col = lax.rem(step, width // tile)
            piece = pl.ds(pl.multiple_of(row * sum_rows, sum_rows), sum_rows)
            columns = pl.ds(pl.multiple_of(col * tile, tile), tile)
            own_sums[layer, index, piece, columns] = jnp.dot(
                lat_rows[piece, :], panel[layer, :, columns], preferred_element_type=F32
            )
            return carry

        lax.fori_loop(0, (lat_count // sum_rows) * (width // tile), chunk, 0)

    def project_queries(layer):
        def chunk(col, carry):
            columns = pl.ds(pl.multiple_of(col * tile, tile), tile)
            sums = jnp.dot(normed[...], wq[layer, :, columns], preferred_element_type=F32)
            query_rows[:, columns] = (sums * scale).astype(BF16)
            return carry

        lax.fori_loop(0, width // tile, chunk, 0)

    def project_output(layer, target):
        def chunk(col, carry):
            columns = pl.ds(pl.multiple_of(col * tile, tile), tile)
            sums = jnp.dot(attended[...], wo[layer, :, columns], preferred_element_type=F32)
            target[:, columns] = (hidden[:, columns].astype(F32) + sums).astype(BF16)
            return carry

        lax.fori_loop(0, width // tile, chunk, 0)

    attend_rows = rows if lat_count <= 256 else min(rows, 128)

    def attend(layer):
        first = lax.broadcasted_iota(jnp.int32, (lat_count, pair), 1) < head_size
        zeros = jnp.zeros((lat_count, pair), F32)
        ones = jnp.ones((lat_count, pair), F32)
        counts = jnp.concatenate(
            [jnp.where(first, ones, zeros), jnp.where(first, zeros, ones)], axis=0
        ).astype(BF16)

        def heads(index, carry):
            columns = pl.ds(pl.multiple_of(index * pair, pair), pair)
            keys = own_sums[layer, 0, :, columns] + peer_sums[layer, 0, :, columns]
            values = own_sums[layer, 1, :, columns] + peer_sums[layer, 1, :, columns]
            key_block = jnp.concatenate(
                [jnp.where(first, keys, zeros), jnp.where(first, zeros, keys)], axis=0
            ).astype(BF16)
            value_block = jnp.concatenate(
                [jnp.where(first, values, zeros), jnp.where(first, zeros, values)], axis=0
            ).astype(BF16)
            value_block = jnp.concatenate([value_block, counts], axis=1)

            def row_chunk(step, inner):
                piece = pl.ds(pl.multiple_of(step * attend_rows, attend_rows), attend_rows)
                scores = lax.dot_general(
                    query_rows[piece, columns],
                    key_block,
                    (((1,), (1,)), ((), ())),
                    preferred_element_type=F32,
                )
                probs = []
                for side in range(2):
                    part = scores[:, side * lat_count : (side + 1) * lat_count]
                    row_max = jnp.max(part, axis=-1, keepdims=True)
                    probs.append(jnp.exp(part - row_max).astype(BF16))
                mixed = jnp.dot(
                    jnp.concatenate(probs, axis=1), value_block, preferred_element_type=F32
                )
                attended[piece, columns] = (mixed[:, :pair] / mixed[:, pair:]).astype(BF16)
                return inner

            if attend_rows == rows:
                row_chunk(0, 0)
            else:
                lax.fori_loop(0, rows // attend_rows, row_chunk, 0)
            return carry

        lax.fori_loop(0, HEADS // 2, heads, 0)

    local[0].wait()
    layer_norm(0)

    own_latents.wait()

    def take_latents(step, carry):
        source = lax.rem(me + devices - step, devices)
        pltpu.make_async_remote_copy(
            src_ref=lat.at[source],
            dst_ref=lat.at[source],
            send_sem=lat_send_sem.at[step],
            recv_sem=lat_recv_sem.at[source],
            device_id=peer,
            device_id_type=MESH,
        ).wait_recv()
        return carry

    lax.fori_loop(1, devices, take_latents, 0)
    lat_rows[...] = lat[...].astype(F32).reshape(lat_count, half).astype(BF16)

    for layer in range(LAYERS):
        for index in range(2):
            own["kv"[index], layer].wait()
            project_latents(index, layer)
            sums_copy(index, layer).start()
        weight_copy(1, layer).start()
        if layer + 1 < LAYERS:
            weight_copy(0, layer + 1).start()

    for layer in range(LAYERS):
        if layer > 0:
            layer_norm(layer)
        own["q", layer].wait()
        weight_wait(weight_recv_sem, wq, 0, layer, n, half, weight_send_sem, peer)
        project_queries(layer)
        sums_copy(0, layer).wait_recv()
        sums_copy(1, layer).wait_recv()
        attend(layer)
        own["o", layer].wait()
        weight_wait(weight_recv_sem, wo, 1, layer, n, half, weight_send_sem, peer)
        project_output(layer, out if layer == LAYERS - 1 else hidden)

    def finish_latents(step, carry):
        latent_copy(step).wait_send()
        return carry

    lax.fori_loop(1, devices, finish_latents, 0)
    for layer in range(LAYERS):
        for index in range(2):
            weight_copy(index, layer).wait_send()
            sums_copy(index, layer).wait_send()


def weight_wait(recv_sem, target, index, layer, n, half, send_sem, peer):
    other_half = pl.ds(pl.multiple_of((1 - n) * half, half), half)
    pltpu.make_async_remote_copy(
        src_ref=target.at[layer, other_half],
        dst_ref=target.at[layer, other_half],
        send_sem=send_sem.at[index, layer],
        recv_sem=recv_sem.at[index, layer],
        device_id=peer,
        device_id_type=MESH,
    ).wait_recv()


def shards(wide, narrow, queries, latents, norm_gains, q_weight, k_weight, v_weight, o_weight):
    rows, width = queries.shape
    devices = wide * narrow
    lat_piece = latents.shape[0]
    lat_count = devices * lat_piece
    half = k_weight.shape[1]
    anywhere = pl.BlockSpec(memory_space=pl.ANY)
    vmem = pl.BlockSpec(memory_space=pltpu.VMEM)
    dma = pltpu.SemaphoreType.DMA
    return pl.pallas_call(
        functools.partial(decoder, wide, narrow),
        out_shape=jax.ShapeDtypeStruct((rows, width), BF16),
        in_specs=[anywhere, anywhere, vmem, anywhere, anywhere, anywhere, anywhere],
        out_specs=vmem,
        scratch_shapes=[
            pltpu.VMEM((rows, width), BF16),
            pltpu.VMEM((rows, width), BF16),
            pltpu.VMEM((rows, width), BF16),
            pltpu.VMEM((rows, width), BF16),
            pltpu.VMEM((devices, lat_piece, half), BF16),
            pltpu.VMEM((lat_count, half), BF16),
            pltpu.VMEM((LAYERS, narrow * half, width), BF16),
            pltpu.VMEM((LAYERS, narrow * half, width), BF16),
            pltpu.VMEM((LAYERS, half, width), BF16),
            pltpu.VMEM((LAYERS, half, width), BF16),
            pltpu.VMEM((LAYERS, 2, lat_count, width), F32),
            pltpu.VMEM((LAYERS, 2, lat_count, width), F32),
            dma,
            dma,
            dma((4, LAYERS)),
            dma((devices,)),
            dma((devices,)),
            dma((2, LAYERS)),
            dma((2, LAYERS)),
            dma((2, LAYERS)),
            dma((2, LAYERS)),
        ],
        compiler_params=pltpu.CompilerParams(
            collective_id=0,
            has_side_effects=True,
            vmem_limit_bytes=60 * 1024 * 1024,
        ),
    )(queries, latents, norm_gains, q_weight, k_weight, v_weight, o_weight)


def solution(mesh):
    rows = P(("groups", "wide", "narrow"), None)
    panel = P(None, "narrow", None)
    return jax.shard_map(
        functools.partial(shards, mesh.shape["wide"], mesh.shape["narrow"]),
        mesh=mesh,
        in_specs=(rows, rows, P(), panel, panel, panel, panel),
        out_specs=rows,
        check_vma=False,
    )
```

time: 127 us -> 33.6 us (0.26)
  waiting for transfers between devices: 42.4 us -> 0 us
  Pallas kernels: 0 us -> 31.1 us
  matrix products: 29.1 us -> 0 us
  blocking collectives: 23.8 us -> 0 us
  between operations: 13.7 us -> 0.01 us
  local copies, waits for them, and re-layouts: 14.9 us -> 2.26 us
  other arithmetic: 2.53 us -> 0 us
    all_gather x8 -> x0, waiting for transfers between devices: 39.9 us -> none  [the longest x2 15.5 us: project_output(): lax.all_gather(panel, 'narrow', axis=0, tiled=True)]
    pallas_call x0 -> x1, Pallas kernels: none -> 31.1 us  [shards(): pl.pallas_call(functools.partial(decoder, wide, narrow), out_shape=jax.Sh...]
    dot_general x12 -> x0, matrix products: 29.1 us -> none  [the longest x8 22.5 us: accumulate(): return jnp.dot(left_rows, panel_piece, preferred_element_type=jnp.float32)]
    all_gather x1 -> x0, blocking collectives: 23.8 us -> none  [shards(): lax.all_gather(latents, ('wide', 'narrow'), axis=0, tiled=True)]
    slice x5 -> x0, local copies, waits for them, and re-layouts: 9.26 us -> none  [the longest x1 3.22 us: shards(): v_weight[layer_index]]
    convert_element_type x6 -> x0, local copies, waits for them, and re-layouts: 3.41 us -> none  [the longest x2 2.04 us: shards(): query_rows = (query_sums * score_scale).astype(jnp.bfloat16)]
    unnamed x8 -> x0, waiting for transfers between devices: 2.5 us -> none
    reduce_sum x5 -> x0, other arithmetic: 2.44 us -> none  [the longest x2 1.38 us: fold_step(): row_sum = row_sum * rescale + jnp.sum(expo, axis=-1)]
  transfers between devices with their start and end apart: 8 -> 0, of which waited for: 5 -> 0; matrix products, arithmetic and copies ran while one was open for 29% -> 0% of each run, Pallas kernels for 0% -> 0%
where the time goes in v1:
time: 33.6 us; the launch traced here: 33.4 us
  Pallas kernels  31.1 us (93%)
  local copies, waits for them, and re-layouts  2.26 us (7%)
    pallas_call x1, Pallas kernels, shards(): pl.pallas_call(functools.partial(decoder, wide, narrow), out_shape=jax.Sh...  31.1 us
    unnamed x1, local copies, waits for them, and re-layouts  2.26 us

profile of v1, /device:TPU:0, one launch (start us, length us, event | category | flops | bytes accessed | tf_op | source)
XLA Modules:
  0.0 33.4 jit_solution(16196607811924367439)
XLA Ops:
  0.0 31.1 %shard_map.73 = bf16[512,1024]{1,0:T(8,128)(2,1)} custom-call(bf16[512,1024]{1,0:T(8,128)(2,1)} %queries.1, bf16[8,1024]{1,0:T(8,128)(2,1)} %latents.1, f32[2,1024]{1,0:T(2,128)} %gains.1, bf16[2,512,1024]{2,1,0:T(8,128)(2,1)} %q_weight.1, bf16[2,512,1024]{2,1,0:T(8,128)(2,1)} %k_weight.1, bf16[2,512,1024]{2,1,0:T(8,128)(2,1)} %v_weight.1, ...), custom_call_target="tpu_custom_call" | custom-call | tf_op jit(solution)/shard_map/pallas_call | solution.py:316
  31.1 2.3 %copy.9 = bf16[512,1024]{1,0:T(8,128)(2,1)} copy(bf16[512,1024]{1,0:T(8,128)(2,1)} %shard_map.73) | data formatting | bytes 2097152

commit v2 on v1

--- a/solution.py
+++ b/solution.py
@@ -95,7 +95,6 @@
         return carry
 
     lax.fori_loop(1, devices, greet, 0)
-    pl.semaphore_wait(barrier, devices - 1)
 
     def latent_copy(step):
         other = lax.rem(me + step, devices)
@@ -114,8 +113,6 @@
         latent_copy(step).start()
         return carry
 
-    lax.fori_loop(1, devices, send_latents, 0)
-
     def weight_copy(index, layer):
         source, target = ((q_weight, wq), (o_weight, wo))[index]
         return pltpu.make_async_remote_copy(
@@ -127,17 +124,15 @@
             device_id_type=MESH,
         )
 
-    def sums_copy(index, layer):
+    def sums_copy(layer, col):
         return pltpu.make_async_remote_copy(
-            src_ref=own_sums.at[layer, index],
-            dst_ref=peer_sums.at[layer, index],
-            send_sem=sums_send_sem.at[index, layer],
-            recv_sem=sums_recv_sem.at[index, layer],
+            src_ref=own_sums.at[layer, col],
+            dst_ref=peer_sums.at[layer, col],
+            send_sem=sums_send_sem.at[layer, col],
+            recv_sem=sums_recv_sem.at[layer, col],
             device_id=peer,
             device_id_type=MESH,
         )
-
-    weight_copy(0, 0).start()
 
     norm_rows = min(rows, 128)
 
@@ -156,21 +151,20 @@
 
     sum_rows = min(lat_count, 256)
     tile = 256
-
-    def project_latents(index, layer):
-        panel = (wk, wv)[index]
+    tiles = width // tile
+
+    def project_latents(layer, col):
+        columns = pl.ds(col * tile, tile)
 
         def chunk(step, carry):
-            row = step // (width // tile)
-            col = lax.rem(step, width // tile)
-            piece = pl.ds(pl.multiple_of(row * sum_rows, sum_rows), sum_rows)
-            columns = pl.ds(pl.multiple_of(col * tile, tile), tile)
-            own_sums[layer, index, piece, columns] = jnp.dot(
-                lat_rows[piece, :], panel[layer, :, columns], preferred_element_type=F32
-            )
-            return carry
-
-        lax.fori_loop(0, (lat_count // sum_rows) * (width // tile), chunk, 0)
+            piece = pl.ds(step * sum_rows if isinstance(step, int) else pl.multiple_of(step * sum_rows, sum_rows), sum_rows)
+            for index in range(2):
+                own_sums[layer, col, index, piece, :] = jnp.dot(
+                    lat_rows[piece, :], (wk, wv)[index][layer, :, columns], preferred_element_type=F32
+                )
+            return carry
+
+        loop(lat_count // sum_rows, chunk)
 
     def project_queries(layer):
         def chunk(col, carry):
@@ -190,57 +184,57 @@
 
         lax.fori_loop(0, width // tile, chunk, 0)
 
-    attend_rows = rows if lat_count <= 256 else min(rows, 128)
-
-    def attend(layer):
-        first = lax.broadcasted_iota(jnp.int32, (lat_count, pair), 1) < head_size
-        zeros = jnp.zeros((lat_count, pair), F32)
-        ones = jnp.ones((lat_count, pair), F32)
-        counts = jnp.concatenate(
-            [jnp.where(first, ones, zeros), jnp.where(first, zeros, ones)], axis=0
+    attend_rows = min(rows, 256 if lat_count <= 256 else 128)
+    first = lax.broadcasted_iota(jnp.int32, (lat_count, pair), 1) < head_size
+    zeros = jnp.zeros((lat_count, pair), F32)
+    ones = jnp.ones((lat_count, pair), F32)
+    counts = jnp.concatenate(
+        [jnp.where(first, ones, zeros), jnp.where(first, zeros, ones)], axis=0
+    ).astype(BF16)
+
+    def attend_pair(layer, col, at):
+        columns = pl.ds(col * tile + at, pair)
+        keys = own_sums[layer, col, 0, :, at : at + pair] + peer_sums[layer, col, 0, :, at : at + pair]
+        values = own_sums[layer, col, 1, :, at : at + pair] + peer_sums[layer, col, 1, :, at : at + pair]
+        key_block = jnp.concatenate(
+            [jnp.where(first, keys, zeros), jnp.where(first, zeros, keys)], axis=0
         ).astype(BF16)
-
-        def heads(index, carry):
-            columns = pl.ds(pl.multiple_of(index * pair, pair), pair)
-            keys = own_sums[layer, 0, :, columns] + peer_sums[layer, 0, :, columns]
-            values = own_sums[layer, 1, :, columns] + peer_sums[layer, 1, :, columns]
-            key_block = jnp.concatenate(
-                [jnp.where(first, keys, zeros), jnp.where(first, zeros, keys)], axis=0
-            ).astype(BF16)
-            value_block = jnp.concatenate(
-                [jnp.where(first, values, zeros), jnp.where(first, zeros, values)], axis=0
-            ).astype(BF16)
-            value_block = jnp.concatenate([value_block, counts], axis=1)
-
-            def row_chunk(step, inner):
-                piece = pl.ds(pl.multiple_of(step * attend_rows, attend_rows), attend_rows)
-                scores = lax.dot_general(
-                    query_rows[piece, columns],
-                    key_block,
-                    (((1,), (1,)), ((), ())),
-                    preferred_element_type=F32,
-                )
-                probs = []
-                for side in range(2):
-                    part = scores[:, side * lat_count : (side + 1) * lat_count]
-                    row_max = jnp.max(part, axis=-1, keepdims=True)
-                    probs.append(jnp.exp(part - row_max).astype(BF16))
-                mixed = jnp.dot(
-                    jnp.concatenate(probs, axis=1), value_block, preferred_element_type=F32
-                )
-                attended[piece, columns] = (mixed[:, :pair] / mixed[:, pair:]).astype(BF16)
-                return inner
-
-            if attend_rows == rows:
-                row_chunk(0, 0)
-            else:
-                lax.fori_loop(0, rows // attend_rows, row_chunk, 0)
-            return carry
-
-        lax.fori_loop(0, HEADS // 2, heads, 0)
+        value_block = jnp.concatenate(
+            [jnp.where(first, values, zeros), jnp.where(first, zeros, values)], axis=0
+        ).astype(BF16)
+        value_block = jnp.concatenate([value_block, counts], axis=1)
+
+        def row_chunk(step, carry):
+            piece = pl.ds(step * attend_rows if isinstance(step, int) else pl.multiple_of(step * attend_rows, attend_rows), attend_rows)
+            scores = lax.dot_general(
+                query_rows[piece, columns],
+                key_block,
+                (((1,), (1,)), ((), ())),
+                preferred_element_type=F32,
+            )
+            probs = []
+            for side in range(2):
+                part = scores[:, side * lat_count : (side + 1) * lat_count]
+                row_max = jnp.max(part, axis=-1, keepdims=True)
+                probs.append(jnp.exp(part - row_max).astype(BF16))
+            mixed = jnp.dot(
+                jnp.concatenate(probs, axis=1), value_block, preferred_element_type=F32
+            )
+            attended[piece, columns] = (mixed[:, :pair] / mixed[:, pair:]).astype(BF16)
+            return carry
+
+        loop(rows // attend_rows, row_chunk)
 
     local[0].wait()
     layer_norm(0)
+    pl.semaphore_wait(barrier, devices - 1)
+    lax.fori_loop(1, devices, send_latents, 0)
+    weight_copy(0, 0).start()
+
+    own["q", 0].wait()
+    weight_wait(weight_recv_sem, wq, 0, 0, n, half, weight_send_sem, peer)
+    weight_copy(1, 0).start()
+    project_queries(0)
 
     own_latents.wait()
 
@@ -260,23 +254,28 @@
     lat_rows[...] = lat[...].astype(F32).reshape(lat_count, half).astype(BF16)
 
     for layer in range(LAYERS):
-        for index in range(2):
-            own["kv"[index], layer].wait()
-            project_latents(index, layer)
-            sums_copy(index, layer).start()
-        weight_copy(1, layer).start()
-        if layer + 1 < LAYERS:
-            weight_copy(0, layer + 1).start()
+        own["k", layer].wait()
+        own["v", layer].wait()
+        for col in range(tiles):
+            project_latents(layer, col)
+            if layer == 0:
+                sums_copy(layer, col).start()
 
     for layer in range(LAYERS):
         if layer > 0:
             layer_norm(layer)
-        own["q", layer].wait()
-        weight_wait(weight_recv_sem, wq, 0, layer, n, half, weight_send_sem, peer)
-        project_queries(layer)
-        sums_copy(0, layer).wait_recv()
-        sums_copy(1, layer).wait_recv()
-        attend(layer)
+            own["q", layer].wait()
+            weight_wait(weight_recv_sem, wq, 0, layer, n, half, weight_send_sem, peer)
+            project_queries(layer)
+        for col in range(tiles):
+            sums_copy(layer, col).wait_recv()
+            if col == tiles // 2 and layer + 1 < LAYERS:
+                weight_copy(0, layer + 1).start()
+                for later in range(tiles):
+                    sums_copy(layer + 1, later).start()
+                weight_copy(1, layer + 1).start()
+            for at in range(0, tile, pair):
+                attend_pair(layer, col, at)
         own["o", layer].wait()
         weight_wait(weight_recv_sem, wo, 1, layer, n, half, weight_send_sem, peer)
         project_output(layer, out if layer == LAYERS - 1 else hidden)
@@ -289,7 +288,16 @@
     for layer in range(LAYERS):
         for index in range(2):
             weight_copy(index, layer).wait_send()
-            sums_copy(index, layer).wait_send()
+        for col in range(tiles):
+            sums_copy(layer, col).wait_send()
+
+
+def loop(count, body):
+    if count <= 2:
+        for step in range(count):
+            body(step, 0)
+    else:
+        lax.fori_loop(0, count, body, 0)
 
 
 def weight_wait(recv_sem, target, index, layer, n, half, send_sem, peer):
@@ -329,8 +337,8 @@
             pltpu.VMEM((LAYERS, narrow * half, width), BF16),
             pltpu.VMEM((LAYERS, half, width), BF16),
             pltpu.VMEM((LAYERS, half, width), BF16),
-            pltpu.VMEM((LAYERS, 2, lat_count, width), F32),
-            pltpu.VMEM((LAYERS, 2, lat_count, width), F32),
+            pltpu.VMEM((LAYERS, width // 256, 2, lat_count, 256), F32),
+            pltpu.VMEM((LAYERS, width // 256, 2, lat_count, 256), F32),
             dma,
             dma,
             dma((4, LAYERS)),
@@ -338,8 +346,8 @@
             dma((devices,)),
             dma((2, LAYERS)),
             dma((2, LAYERS)),
-            dma((2, LAYERS)),
-            dma((2, LAYERS)),
+            dma((LAYERS, width // 256)),
+            dma((LAYERS, width // 256)),
         ],
         compiler_params=pltpu.CompilerParams(
             collective_id=0,

time: 33.6 us -> 28.7 us (0.85)
  Pallas kernels: 31.1 us -> 26.2 us
    pallas_call x1, Pallas kernels: 31.1 us -> 26.2 us  [shards(): pl.pallas_call(functools.partial(decoder, wide, narrow), out_shape=jax.Sh...]
where the time goes in v2:
time: 28.7 us; the launch traced here: 28.5 us
  Pallas kernels  26.2 us (91%)
  local copies, waits for them, and re-layouts  2.26 us (8%)
    pallas_call x1, Pallas kernels, shards(): pl.pallas_call(functools.partial(decoder, wide, narrow), out_shape=jax.Sh...  26.2 us
    unnamed x1, local copies, waits for them, and re-layouts  2.26 us

profile of v2, /device:TPU:0, one launch (start us, length us, event | category | flops | bytes accessed | tf_op | source)
XLA Modules:
  0.0 28.5 jit_solution(9730225744122840182)
XLA Ops:
  0.0 26.2 %shard_map.73 = bf16[512,1024]{1,0:T(8,128)(2,1)} custom-call(bf16[512,1024]{1,0:T(8,128)(2,1)} %queries.1, bf16[8,1024]{1,0:T(8,128)(2,1)} %latents.1, f32[2,1024]{1,0:T(2,128)} %gains.1, bf16[2,512,1024]{2,1,0:T(8,128)(2,1)} %q_weight.1, bf16[2,512,1024]{2,1,0:T(8,128)(2,1)} %k_weight.1, bf16[2,512,1024]{2,1,0:T(8,128)(2,1)} %v_weight.1, ...), custom_call_target="tpu_custom_call" | custom-call | tf_op jit(solution)/shard_map/pallas_call | solution.py:324
  26.3 2.3 %copy.9 = bf16[512,1024]{1,0:T(8,128)(2,1)} copy(bf16[512,1024]{1,0:T(8,128)(2,1)} %shard_map.73) | data formatting | bytes 2097152

commit v3 on v2

--- a/solution.py
+++ b/solution.py
@@ -46,6 +46,7 @@
     weight_recv_sem,
     sums_send_sem,
     sums_recv_sem,
+    out_sem,
 ):
     devices = wide * narrow
     w = lax.axis_index("wide")
@@ -175,14 +176,17 @@
 
         lax.fori_loop(0, width // tile, chunk, 0)
 
-    def project_output(layer, target):
-        def chunk(col, carry):
-            columns = pl.ds(pl.multiple_of(col * tile, tile), tile)
+    def out_copy(col):
+        columns = pl.ds(col * tile, tile)
+        return pltpu.make_async_copy(hidden.at[:, columns], out.at[:, columns], out_sem.at[col])
+
+    def project_output(layer):
+        for col in range(tiles):
+            columns = pl.ds(col * tile, tile)
             sums = jnp.dot(attended[...], wo[layer, :, columns], preferred_element_type=F32)
-            target[:, columns] = (hidden[:, columns].astype(F32) + sums).astype(BF16)
-            return carry
-
-        lax.fori_loop(0, width // tile, chunk, 0)
+            hidden[:, columns] = (hidden[:, columns].astype(F32) + sums).astype(BF16)
+            if layer == LAYERS - 1:
+                out_copy(col).start()
 
     attend_rows = min(rows, 256 if lat_count <= 256 else 128)
     first = lax.broadcasted_iota(jnp.int32, (lat_count, pair), 1) < head_size
@@ -278,7 +282,7 @@
                 attend_pair(layer, col, at)
         own["o", layer].wait()
         weight_wait(weight_recv_sem, wo, 1, layer, n, half, weight_send_sem, peer)
-        project_output(layer, out if layer == LAYERS - 1 else hidden)
+        project_output(layer)
 
     def finish_latents(step, carry):
         latent_copy(step).wait_send()
@@ -290,6 +294,8 @@
             weight_copy(index, layer).wait_send()
         for col in range(tiles):
             sums_copy(layer, col).wait_send()
+    for col in range(tiles):
+        out_copy(col).wait()
 
 
 def loop(count, body):
@@ -325,7 +331,7 @@
         functools.partial(decoder, wide, narrow),
         out_shape=jax.ShapeDtypeStruct((rows, width), BF16),
         in_specs=[anywhere, anywhere, vmem, anywhere, anywhere, anywhere, anywhere],
-        out_specs=vmem,
+        out_specs=anywhere,
         scratch_shapes=[
             pltpu.VMEM((rows, width), BF16),
             pltpu.VMEM((rows, width), BF16),
@@ -348,6 +354,7 @@
             dma((2, LAYERS)),
             dma((LAYERS, width // 256)),
             dma((LAYERS, width // 256)),
+            dma((width // 256,)),
         ],
         compiler_params=pltpu.CompilerParams(
             collective_id=0,

time: 28.7 us -> 28 us (0.976)
  Pallas kernels: 26.2 us -> 25.5 us
    pallas_call x1, Pallas kernels: 26.2 us -> 25.5 us  [shards(): pl.pallas_call(functools.partial(decoder, wide, narrow), out_shape=jax.Sh...]
where the time goes in v3:
time: 28 us; the launch traced here: 27.8 us
  Pallas kernels  25.5 us (91%)
  local copies, waits for them, and re-layouts  2.26 us (8%)
    pallas_call x1, Pallas kernels, shards(): pl.pallas_call(functools.partial(decoder, wide, narrow), out_shape=jax.Sh...  25.5 us
    unnamed x1, local copies, waits for them, and re-layouts  2.26 us

profile of v3, /device:TPU:0, one launch (start us, length us, event | category | flops | bytes accessed | tf_op | source)
XLA Modules:
  0.0 27.8 jit_solution(16116723485097394175)
XLA Ops:
  0.0 25.5 %shard_map.73 = bf16[512,1024]{1,0:T(8,128)(2,1)} custom-call(bf16[512,1024]{1,0:T(8,128)(2,1)} %queries.1, bf16[8,1024]{1,0:T(8,128)(2,1)} %latents.1, f32[2,1024]{1,0:T(2,128)} %gains.1, bf16[2,512,1024]{2,1,0:T(8,128)(2,1)} %q_weight.1, bf16[2,512,1024]{2,1,0:T(8,128)(2,1)} %k_weight.1, bf16[2,512,1024]{2,1,0:T(8,128)(2,1)} %v_weight.1, ...), custom_call_target="tpu_custom_call" | custom-call | tf_op jit(solution)/shard_map/pallas_call | solution.py:330
  25.5 2.3 %copy.9 = bf16[512,1024]{1,0:T(8,128)(2,1)} copy(bf16[512,1024]{1,0:T(8,128)(2,1)} %shard_map.73) | data formatting | bytes 2097152
